TPU v7x, 32 devices: a whole 2x2x4 slice. The times are simulated.
32 devices in a mesh: dp: 4 (over z), ctx: 4 (over y, x), tensor: 2 (over core).
Axes of the slice: x: 2, y: 2, z: 4, core: 2. Of those that a mesh axis runs over, the one named last changes fastest.
Arguments:
- tokens: bfloat16 [12, 1024, 768], P('dp', 'ctx'), may hold values from -6 to 6
- segment_ids: int32 [12, 1024], P('dp', 'ctx'), may hold values from 0 to 3, never falling along the last dimension, each value on 1 to 512 neighbouring positions
- w_qkv: bfloat16 [3, 768, 768], P(None, None, 'tensor'), may hold values from -0.21875 to 0.21875
- w_out: bfloat16 [768, 768], P('tensor'), may hold values from -3 to 3
- w_up: bfloat16 [3072, 768], P('tensor'), may hold values from -0.21875 to 0.21875
- w_down: bfloat16 [3072, 768], P('tensor'), may hold values from -0.109375 to 0.109375
- norm_gain: float32 [2, 768], replicated, may hold values from 0.1 to 1.9
- norm_bias: float32 [2, 768], replicated, may hold values from -1.5 to 1.5
- grad_out: bfloat16 [12, 1024, 768], P('dp', 'ctx'), may hold values from -6 to 6
Outputs:
- out: bfloat16 [12, 1024, 768], P('dp', 'ctx')
- grad_tokens: float32 [12, 1024, 768], P('dp', 'ctx')
- grad_qkv: float32 [3, 768, 768], P(None, 'ctx', 'tensor')
- grad_w_out: float32 [768, 768], P('tensor', 'ctx')
- grad_up: float32 [3072, 768], P('tensor', 'ctx')
- grad_down: float32 [3072, 768], P('tensor', 'ctx')
- grad_gain: float32 [2, 768], P(None, 'ctx')
- grad_bias: float32 [2, 768], P(None, 'ctx')
Inputs may be any that keep to these rules, and one draw needn't show every extreme that they name: `segment_ids`: documents are contiguous runs of equal ids that never fall along a sequence; each id names 1 to 512 tokens and one document has exactly 512.
All inputs are finite; a program needn't handle non-finite values.
Results may differ from a plain program's by a relative error of at most 0.02.
Values may be sent and summed in bfloat16 or wider, within the bound.
No kernel may reach another device: no remote copies, remote signals or barrier semaphores. Data moves between devices by JAX's collectives and lax.ppermute only.
A program may use at most 320 MiB of HBM per device.

v0:
```python
import jax
import jax.numpy as jnp
from jax import lax
from jax.sharding import PartitionSpec as P

HEAD_DIM = 64
neg_big = -1e30
dims_rows = (((0,), (0,)), ((), ()))
dims_cols = (((1,), (1,)), ((), ()))


def layer_norm(residual, norm_gain, norm_shift):
    center = residual - jnp.mean(residual, axis=-1, keepdims=True)
    spread = jnp.mean(center * center, axis=-1, keepdims=True)
    return center * lax.rsqrt(spread + 1e-06) * norm_gain + norm_shift


def gelu_exact(values):
    return jax.nn.gelu(values, approximate=False)


def scores_of(queries, key_heads):
    return (
        jnp.einsum("sqhd,skhd->shqk", queries, key_heads, preferred_element_type=jnp.float32)
        * 0.125
    )


def score_grads(
    queries, d_heads, lse_query, delta_query, seg_query, key_heads, value_heads, seg_keys
):
    allowed = seg_query[:, None, :, None] == seg_keys[:, None, None, :]
    weights = jnp.where(allowed, jnp.exp(scores_of(queries, key_heads) - lse_query[..., None]), 0.0)
    d_weights = jnp.einsum(
        "sqhd,skhd->shqk", d_heads, value_heads, preferred_element_type=jnp.float32
    )
    d_scores = (weights * (d_weights - delta_query[..., None])).astype(jnp.bfloat16)
    return (weights, d_scores)


def key_grads(queries, d_heads, weights, d_scores):
    grad_keys = (
        jnp.einsum("shqk,sqhd->kshd", d_scores, queries, preferred_element_type=jnp.float32) * 0.125
    )
    grad_values = jnp.einsum(
        "shqk,sqhd->kshd", weights.astype(jnp.bfloat16), d_heads, preferred_element_type=jnp.float32
    )
    return (grad_keys, grad_values)


def on_device(tokens, segment_ids, w_qkv, w_out, w_up, w_down, norm_gain, norm_bias, grad_out):
    seq_count, span_rows, model_width = tokens.shape
    local_width = w_out.shape[0]
    local_heads = local_width // HEAD_DIM
    tok_rows = seq_count * span_rows
    flat_tokens = tokens.reshape(tok_rows, model_width)
    projected = jnp.einsum(
        "tf,jfd->jtd", flat_tokens, w_qkv, preferred_element_type=jnp.float32
    ).astype(jnp.bfloat16)
    queries = projected[0].reshape(seq_count, span_rows, local_heads, HEAD_DIM)
    keys_own = projected[1].reshape(seq_count, span_rows, local_width)
    values_own = projected[2].reshape(seq_count, span_rows, local_width)
    packed = jnp.concatenate([keys_own, values_own], axis=-1)
    full_kv, full_seg = (
        lax.all_gather(packed, "ctx", axis=1, tiled=True),
        lax.all_gather(segment_ids, "ctx", axis=1, tiled=True),
    )
    length = full_seg.shape[1]
    key_block = 1024
    block_count = length // key_block

    def key_piece(step_index):
        offset = step_index * key_block
        kv_piece = lax.dynamic_slice_in_dim(full_kv, offset, key_block, 1).reshape(
            seq_count, key_block, 2, local_heads, HEAD_DIM
        )
        seg_piece = lax.dynamic_slice_in_dim(full_seg, offset, key_block, 1)
        allowed = segment_ids[:, None, :, None] == seg_piece[:, None, None, :]
        return (kv_piece[:, :, 0], kv_piece[:, :, 1], allowed, seg_piece)

    def stats_step(step_index, running):
        row_max, row_sum = running
        key_heads, value_heads, allowed, seg_piece = key_piece(step_index)
        scores = jnp.where(allowed, scores_of(queries, key_heads), neg_big)
        new_max = jnp.maximum(row_max, jnp.max(scores, axis=-1))
        row_sum = row_sum * jnp.exp(row_max - new_max) + jnp.sum(
            jnp.where(allowed, jnp.exp(scores - new_max[..., None]), 0.0), axis=-1
        )
        return (new_max, row_sum)

    stat_shape = (seq_count, local_heads, span_rows)
    row_max, row_sum = lax.fori_loop(
        0,
        block_count,
        stats_step,
        (jnp.full(stat_shape, neg_big, jnp.float32), jnp.zeros(stat_shape, jnp.float32)),
    )
    log_total = row_max + jnp.log(row_sum)

    def mix_step(step_index, running):
        key_heads, value_heads, allowed, seg_piece = key_piece(step_index)
        weights = jnp.where(
            allowed, jnp.exp(scores_of(queries, key_heads) - log_total[..., None]), 0.0
        )
        return running + jnp.einsum(
            "shqk,skhd->sqhd",
            weights.astype(jnp.bfloat16),
            value_heads,
            preferred_element_type=jnp.float32,
        )

    head_shape = (seq_count, span_rows, local_heads, HEAD_DIM)
    mixed_float = lax.fori_loop(0, block_count, mix_step, jnp.zeros(head_shape, jnp.float32))
    mixed_heads = mixed_float.astype(jnp.bfloat16).reshape(tok_rows, local_width)
    attention = lax.psum(
        jnp.dot(mixed_heads, w_out, preferred_element_type=jnp.float32).astype(jnp.bfloat16),
        "tensor",
    ).astype(jnp.float32)
    resid_one = flat_tokens.astype(jnp.float32) + attention
    normed_one = layer_norm(resid_one, norm_gain[0], norm_bias[0])
    normed_low = normed_one.astype(jnp.bfloat16)
    upward = lax.dot_general(normed_low, w_up, dims_cols, preferred_element_type=jnp.float32)
    active = gelu_exact(upward).astype(jnp.bfloat16)
    ffn_out = lax.psum(
        jnp.dot(active, w_down, preferred_element_type=jnp.float32).astype(jnp.bfloat16), "tensor"
    ).astype(jnp.float32)
    resid_two = normed_one + ffn_out
    result, norm_back_two = jax.vjp(layer_norm, resid_two, norm_gain[1], norm_bias[1])
    outputs = result.astype(jnp.bfloat16).reshape(seq_count, span_rows, model_width)
    d_resid_two, d_gain_two, d_bias_two = norm_back_two(
        grad_out.reshape(tok_rows, model_width).astype(jnp.float32)
    )
    d_ffn = d_resid_two.astype(jnp.bfloat16)
    grad_down = lax.dot_general(active, d_ffn, dims_rows, preferred_element_type=jnp.float32)
    d_active = lax.dot_general(d_ffn, w_down, dims_cols, preferred_element_type=jnp.float32)
    gelu_value, gelu_back = jax.vjp(gelu_exact, upward)
    d_up = gelu_back(d_active)[0].astype(jnp.bfloat16)
    grad_up = lax.dot_general(d_up, normed_low, dims_rows, preferred_element_type=jnp.float32)
    d_normed = d_resid_two + lax.psum(
        jnp.dot(d_up, w_up, preferred_element_type=jnp.float32).astype(jnp.bfloat16), "tensor"
    ).astype(jnp.float32)
    norm_value, norm_back_one = jax.vjp(layer_norm, resid_one, norm_gain[0], norm_bias[0])
    d_resid_one, d_gain_one, d_bias_one = norm_back_one(d_normed)
    d_attn = d_resid_one.astype(jnp.bfloat16)
    grad_proj_out = lax.dot_general(
        mixed_heads, d_attn, dims_rows, preferred_element_type=jnp.float32
    )
    d_mixed = (
        lax.dot_general(d_attn, w_out, dims_cols, preferred_element_type=jnp.float32)
        .astype(jnp.bfloat16)
        .reshape(head_shape)
    )
    row_delta = jnp.einsum("sqhd,sqhd->shq", d_mixed.astype(jnp.float32), mixed_float)

    def sender_step(running, step_index):
        key_heads, value_heads, allowed, seg_piece = key_piece(step_index)
        weights, d_scores = score_grads(
            queries, d_mixed, log_total, row_delta, segment_ids, key_heads, value_heads, seg_piece
        )
        running = running + jnp.einsum(
            "shqk,skhd->sqhd", d_scores, key_heads, preferred_element_type=jnp.float32
        )
        grad_keys, grad_values = key_grads(queries, d_mixed, weights, d_scores)
        block_terms = jnp.stack(
            [
                grad_keys.reshape(key_block, seq_count, local_width),
                grad_values.reshape(key_block, seq_count, local_width),
            ],
            axis=2,
        )
        return (running, block_terms)

    query_sum, key_term = lax.scan(
        sender_step, jnp.zeros(head_shape, jnp.float32), jnp.arange(block_count, dtype=jnp.int32)
    )
    key_term = key_term.reshape(length, seq_count, 2, local_width)
    key_grad = lax.psum_scatter(
        key_term.astype(jnp.bfloat16), "ctx", scatter_dimension=0, tiled=True
    ).astype(jnp.float32)
    d_query = (query_sum * 0.125).astype(jnp.bfloat16).reshape(tok_rows, local_width)
    d_keys = key_grad[:, :, 0].astype(jnp.bfloat16)
    d_values = key_grad[:, :, 1].astype(jnp.bfloat16)
    grad_qkv = jnp.stack(
        [
            lax.dot_general(flat_tokens, d_query, dims_rows, preferred_element_type=jnp.float32),
            jnp.einsum("scf,csd->fd", tokens, d_keys, preferred_element_type=jnp.float32),
            jnp.einsum("scf,csd->fd", tokens, d_values, preferred_element_type=jnp.float32),
        ]
    )
    d_query_seq = d_query.reshape(seq_count, span_rows, local_width)
    d_input = (
        jnp.einsum("scd,fd->scf", d_query_seq, w_qkv[0], preferred_element_type=jnp.float32)
        + jnp.einsum("csd,fd->scf", d_keys, w_qkv[1], preferred_element_type=jnp.float32)
        + jnp.einsum("csd,fd->scf", d_values, w_qkv[2], preferred_element_type=jnp.float32)
    )
    grad_tokens = d_resid_one.reshape(seq_count, span_rows, model_width) + lax.psum(
        d_input.astype(jnp.bfloat16), "tensor"
    ).astype(jnp.float32)
    shares = (
        lax.psum_scatter(
            grad_qkv.astype(jnp.bfloat16), "ctx", scatter_dimension=1, tiled=True
        ).astype(jnp.float32),
        lax.psum_scatter(
            grad_proj_out.astype(jnp.bfloat16), "ctx", scatter_dimension=1, tiled=True
        ).astype(jnp.float32),
        lax.psum_scatter(
            grad_up.astype(jnp.bfloat16), "ctx", scatter_dimension=1, tiled=True
        ).astype(jnp.float32),
        lax.psum_scatter(
            grad_down.astype(jnp.bfloat16), "ctx", scatter_dimension=1, tiled=True
        ).astype(jnp.float32),
        lax.psum_scatter(
            jnp.stack([d_gain_one, d_gain_two]).astype(jnp.bfloat16),
            "ctx",
            scatter_dimension=1,
            tiled=True,
        ).astype(jnp.float32),
        lax.psum_scatter(
            jnp.stack([d_bias_one, d_bias_two]).astype(jnp.bfloat16),
            "ctx",
            scatter_dimension=1,
            tiled=True,
        ).astype(jnp.float32),
    )
    totals = (
        lax.psum(shares[0].astype(jnp.bfloat16), "dp").astype(jnp.float32),
        lax.psum(shares[1].astype(jnp.bfloat16), "dp").astype(jnp.float32),
        lax.psum(shares[2].astype(jnp.bfloat16), "dp").astype(jnp.float32),
        lax.psum(shares[3].astype(jnp.bfloat16), "dp").astype(jnp.float32),
        lax.psum(shares[4].astype(jnp.bfloat16), "dp").astype(jnp.float32),
        lax.psum(shares[5].astype(jnp.bfloat16), "dp").astype(jnp.float32),
    )
    return (outputs, grad_tokens, totals[0], totals[1], totals[2], totals[3], totals[4], totals[5])


def solution(mesh):
    return jax.shard_map(
        on_device,
        mesh=mesh,
        in_specs=(
            P("dp", "ctx", None),
            P("dp", "ctx"),
            P(None, None, "tensor"),
            P("tensor", None),
            P("tensor", None),
            P("tensor", None),
            P(),
            P(),
            P("dp", "ctx", None),
        ),
        out_specs=(
            P("dp", "ctx", None),
            P("dp", "ctx", None),
            P(None, "ctx", "tensor"),
            P("tensor", "ctx"),
            P("tensor", "ctx"),
            P("tensor", "ctx"),
            P(None, "ctx"),
            P(None, "ctx"),
        ),
        check_vma=False,
    )
```

profile of v0, /device:TPU:0, one launch (start us, length us, event | category | flops | bytes accessed | tf_op | source)
XLA Modules:
  0.0 660.0 jit_solution(13275955745311117265)
XLA Ops:
  17.3 9.6 %all_gather.7 = s32[3,1024]{1,0:T(4,128)S(1)} all-gather(s32[3,256]{1,0:T(4,128)S(1)} %copy-done.28), channel_id=1, replica_groups=mesh['dp'=4,'ctx'=4,'tensor'=2] {'ctx'}, dimensions={1}, use_global_device_ids=true | all-gather | bytes 15360 | tf_op jit(solution)/shard_map/all_gather | solution.py:66
  27.4 48.7 %all-gather.2.cloned.1.call-done = bf16[3,1024,768]{2,1,0:T(8,128)(2,1)} async-done(((bf16[3,256,768]{2,1,0:T(8,128)(2,1)}), bf16[3,1024,768]{2,1,0:T(8,128)(2,1)}) %all-gather.2.cloned.1.call-update) | async-done | bytes 4718608 | tf_op jit(solution)/shard_map/all_gather | solution.py:65
  76.1 6.7 %copy.50 = bf16[3,1024,768]{1,2,0:T(8,128)(2,1)} copy(bf16[3,1024,768]{2,1,0:T(8,128)(2,1)} %all-gather.2.cloned.1.call-done) | data formatting | bytes 9437184 | tf_op jit(solution)/shard_map/all_gather | solution.py:65
  82.8 5.8 select_reduce_fusion.1
  88.6 6.4 select_reduce_fusion
  95.1 10.0 %bitcast_convert_fusion = (bf16[3,256,6,64]{1,3,2,0:T(8,128)(2,1)S(1)}, f32[3,6,64,256]{3,2,1,0:T(8,128)}) fusion(f32[3,6,256,1024]{3,2,1,0:T(8,128)} %copy-done.2, f32[3,6,256]{2,1,0:T(8,128)S(1)} %log_add_fusion, pred[3,256,1024]{2,1,0:T(8,128)(4,1)S(1)} %broadcast_compare_fusion, bf16[3,1024,2,6,64]{1,4,3,2,0:T(8,128)(2,1)} %bitcast.155), kind=kOutput, calls=%fused_computation.80 | convolution fusion | flops 623149056 | bytes 23808000 | tf_op jit(solution)/shard_map/while/body/eval_jaxpr/shqk,skhd->sqhd/dot_general | solution.py:105
  110.4 18.0 %all-reduce.8.cloned.1.call-done = bf16[768,768]{1,0:T(8,128)(2,1)} async-done(((bf16[768,768]{1,0:T(8,128)(2,1)}), bf16[768,768]{1,0:T(8,128)(2,1)}) %all-reduce.8.cloned.1.call-update) | async-done | bytes 1179664 | tf_op jit(solution)/shard_map/psum | solution.py:115
  130.9 15.0 %multiply_convert_fusion.2 = (bf16[768,1536]{1,0:T(8,128)(2,1)S(1)}, f32[768,1536]{1,0:T(8,128)}, f32[768,1536]{1,0:T(8,128)}) fusion(bf16[1536,768]{1,0:T(8,128)(2,1)S(1)} %copy-done, f32[768,768]{1,0:T(8,128)S(1)} %get-tuple-element.134, f32[768]{0:T(1024)S(1)} %copy-done.30, f32[768]{0:T(1024)S(1)} %get-tuple-element.144, f32[768]{0:T(1024)S(1)} %fusion.46), kind=kOutput, calls=%fused_computation.10 | convolution fusion | flops 1890975744 | bytes 16524288 | tf_op jit(solution)/shard_map/dot_general | solution.py:122
  150.4 21.1 %all-reduce.10.cloned.1.call-done = bf16[768,768]{1,0:T(8,128)(2,1)} async-done(((bf16[768,768]{1,0:T(8,128)(2,1)}), bf16[768,768]{1,0:T(8,128)(2,1)}) %all-reduce.10.cloned.1.call-update) | async-done | bytes 1179664 | tf_op jit(solution)/shard_map/psum | solution.py:124
  179.2 6.5 add_convert_fusion
  190.4 20.9 %all-reduce.12.cloned.1.call-done = bf16[768,768]{1,0:T(8,128)(2,1)} async-done(((bf16[768,768]{1,0:T(8,128)(2,1)}), bf16[768,768]{1,0:T(8,128)(2,1)}) %all-reduce.12.cloned.1.call-update) | async-done | bytes 1179664 | tf_op jit(solution)/shard_map/psum | solution.py:139
  211.3 4.1 fusion.55
  223.8 12.2 %convolution_convert_fusion.2 = bf16[3,6,64,1024]{3,2,1,0:T(8,128)(2,1)} fusion(bf16[3,256,6,64]{1,0,3,2:T(4,128)(2,1)} %reshape.160, f32[3,6,256,1024]{3,2,1,0:T(8,128)} %copy-done.2, f32[3,6,256]{2,1,0:T(8,128)S(1)} %copy-done.25, pred[3,256,1024]{2,1,0:T(8,128)(4,1)} %copy-done.10), kind=kOutput, calls=%fused_computation.55 | convolution fusion | flops 624033792 | bytes 22628352 | tf_op jit(solution)/shard_map/while/body/eval_jaxpr/shqk,sqhd->kshd/dot_general | solution.py:45
  236.2 13.0 %multiply_convert_fusion = bf16[3,6,256,1024]{3,2,1,0:T(8,128)(2,1)} fusion(f32[3,6,256,1024]{3,2,1,0:T(8,128)} %copy-done.2, f32[3,6,256]{2,1,0:T(8,128)S(1)} %fusion.25, f32[3,6,256]{2,1,0:T(8,128)S(1)} %copy-done.25, pred[3,256,1024]{2,1,0:T(8,128)(4,1)} %copy-done.10, bf16[3,1024,2,6,64]{1,4,3,2,0:T(8,128)(2,1)S(1)} %bitcast.159, ...), kind=kOutput, calls=%fused_computation | convolution fusion | flops 632291328 | bytes 32096256 | tf_op jit(solution)/shard_map/while/body/eval_jaxpr/sqhd,skhd->shqk/dot_general | solution.py:34
  249.3 7.1 %multiply_convert_fusion.1 = bf16[3,6,64,1024]{3,2,1,0:T(8,128)(2,1)} fusion(bf16[3,6,256,1024]{3,2,1,0:T(8,128)(2,1)} %multiply_convert_fusion, bf16[3,256,6,64]{1,0,3,2:T(4,128)(2,1)} %reshape_squeeze.11), kind=kOutput, calls=%fused_computation.8 | convolution fusion | flops 606339072 | bytes 12386304 | tf_op jit(solution)/shard_map/while/body/eval_jaxpr/shqk,sqhd->kshd/dot_general | solution.py:43
  256.4 4.3 copy.60
  260.7 4.4 copy.61
  265.0 5.0 pad_maximum_fusion
  270.3 7.4 %fusion.19 = bf16[3,6,64,256]{3,2,1,0:T(8,128)(2,1)S(1)} fusion(bf16[3,6,256,1024]{3,2,1,0:T(8,128)(2,1)} %multiply_convert_fusion, bf16[3,1024,2,6,64]{1,4,3,2,0:T(8,128)(2,1)} %bitcast.156), kind=kOutput, calls=%fused_computation.66 | convolution fusion | flops 604569600 | bytes 12386304 | tf_op jit(solution)/shard_map/while/body/eval_jaxpr/shqk,skhd->sqhd/dot_general | solution.py:160
  279.8 48.6 %reduce-scatter.14.cloned.1.call-done = bf16[256,3,2,384]{3,0,1,2:T(8,128)(2,1)} async-done(((bf16[1024,3,2,384]{3,0,1,2:T(8,128)(2,1)}), bf16[256,3,2,384]{3,0,1,2:T(8,128)(2,1)}) %reduce-scatter.14.cloned.1.call-update) | async-done | bytes 1179664 | tf_op jit(solution)/shard_map/reduce_scatter | solution.py:177
  332.8 5.2 copy.76
  344.8 5.9 convolution_convert_fusion
  351.3 5.3 convolution_convert_fusion.1
  367.5 6.4 reduce-scatter.22.cloned.1.call-done
  376.6 26.1 %reduce-scatter.16.cloned.1.call-done = bf16[384,192]{0,1:T(8,128)(2,1)} async-done(((bf16[384,768]{0,1:T(8,128)(2,1)}), bf16[384,192]{0,1:T(8,128)(2,1)}) %reduce-scatter.16.cloned.1.call-update) | async-done | bytes 147472 | tf_op jit(solution)/shard_map/reduce_scatter | solution.py:203
  402.7 40.4 %reduce-scatter.20.cloned.1.call-done = bf16[1536,192]{0,1:T(8,128)(2,1)} async-done(((bf16[1536,768]{0,1:T(8,128)(2,1)}), bf16[1536,192]{0,1:T(8,128)(2,1)}) %reduce-scatter.20.cloned.1.call-update) | async-done | bytes 589840 | tf_op jit(solution)/shard_map/reduce_scatter | solution.py:209
  443.2 40.5 %reduce-scatter.18.cloned.1.call-done = bf16[1536,192]{0,1:T(8,128)(2,1)} async-done(((bf16[1536,768]{0,1:T(8,128)(2,1)}), bf16[1536,192]{0,1:T(8,128)(2,1)}) %reduce-scatter.18.cloned.1.call-update) | async-done | bytes 589840 | tf_op jit(solution)/shard_map/reduce_scatter | solution.py:206
  483.7 27.2 %reduce-scatter.24.cloned.1.call-done = bf16[192,2]{1,0:T(8,128)(2,1)} async-done(((bf16[768,2]{1,0:T(8,128)(2,1)}), bf16[192,2]{1,0:T(8,128)(2,1)}) %reduce-scatter.24.cloned.1.call-update) | async-done | bytes 784
  511.7 25.9 %reduce-scatter.26.cloned.1.call-done = bf16[192,2]{1,0:T(8,128)(2,1)} async-done(((bf16[768,2]{1,0:T(8,128)(2,1)}), bf16[192,2]{1,0:T(8,128)(2,1)}) %reduce-scatter.26.cloned.1.call-update) | async-done | bytes 784
  538.5 11.7 %all-reduce = (bf16[2,192]{1,0:T(2,128)(2,1)S(1)}, bf16[2,192]{1,0:T(2,128)(2,1)S(1)}) all-reduce(bf16[2,192]{1,0:T(2,128)(2,1)S(1)} %copy.79, bf16[2,192]{1,0:T(2,128)(2,1)S(1)} %copy.81), channel_id=1, replica_groups=mesh['dp'=4,'ctx'=4,'tensor'=2] {'dp'}, use_global_device_ids=true, to_apply=%region_26.27 | all-reduce | flops 768 | bytes 3072 | tf_op jit(solution)/shard_map/psum | solution.py:230
  551.4 8.9 %all-reduce.14.cloned.1.call-done = bf16[3,256,768]{2,1,0:T(8,128)(2,1)} async-done(((bf16[3,256,768]{2,1,0:T(8,128)(2,1)}), bf16[3,256,768]{2,1,0:T(8,128)(2,1)}) %all-reduce.14.cloned.1.call-update) | async-done | bytes 1179664 | tf_op jit(solution)/shard_map/psum | solution.py:196
  563.1 83.4 %all-reduce.16.cloned.1.call-done = (bf16[3,192,384]{1,2,0:T(8,128)(2,1)}, bf16[384,192]{0,1:T(8,128)(2,1)}, bf16[1536,192]{0,1:T(8,128)(2,1)}, bf16[1536,192]{0,1:T(8,128)(2,1)}) async-done(((bf16[3,192,384]{1,2,0:T(8,128)(2,1)}, bf16[384,192]{0,1:T(8,128)(2,1)}, bf16[1536,192]{0,1:T(8,128)(2,1)}, bf16[1536,192]{0,1:T(8,128)(2,1)}), (bf16[3,192,384]{1,2,0:T(8,128)(2,1)}, bf16[384,192]{0,1:T(8,128)(2,1)}, ...) | async-done | bytes 1769488 | tf_op jit(solution)/shard_map/psum | solution.py:226
  (176 shorter events, 83.3 us)
Async XLA Ops:
  7.2 123.7 %copy-start = (bf16[1536,768]{1,0:T(8,128)(2,1)S(1)}, bf16[1536,768]{1,0:T(8,128)(2,1)}, u32[]{:S(2)}) copy-start(bf16[1536,768]{1,0:T(8,128)(2,1)} %param.13) | copy-start | bytes 7077892
  7.2 68.9 %all-gather.2.cloned.1.call-start = ((), (), s32[]{:S(2)}) async-start(), calls=%async_computation.7 | async-start | bytes 5898240 | tf_op jit(solution)/shard_map/all_gather | solution.py:65
  16.2 112.2 %all-reduce.8.cloned.1.call-start = ((), (), s32[]{:S(2)}) async-start(), calls=%async_computation.8 | async-start | bytes 2359296 | tf_op jit(solution)/shard_map/psum | solution.py:115
  27.4 67.6 %copy-start.10 = (pred[3,256,1024]{2,1,0:T(8,128)(4,1)}, pred[3,256,1024]{2,1,0:T(8,128)(4,1)S(1)}, u32[]{:S(2)}) copy-start(pred[3,256,1024]{2,1,0:T(8,128)(4,1)S(1)} %broadcast_compare_fusion) | copy-start | bytes 2359300
  88.6 6.5 copy-start.2
  95.1 10.1 %copy-start.24 = (f32[3,6,256]{2,1,0:T(8,128)}, f32[3,6,256]{2,1,0:T(8,128)S(1)}, u32[]{:S(2)}) copy-start(f32[3,6,256]{2,1,0:T(8,128)S(1)} %log_add_fusion) | copy-start | bytes 55300
  105.6 22.8 %copy-start.11 = (bf16[3,256,768]{2,1,0:T(8,128)(2,1)S(1)}, bf16[3,256,768]{2,1,0:T(8,128)(2,1)}, u32[]{:S(2)}) copy-start(bf16[3,256,768]{2,1,0:T(8,128)(2,1)} %param.9) | copy-start | bytes 3538948
  108.4 63.0 %all-reduce.10.cloned.1.call-start = ((), (), s32[]{:S(2)}) async-start(), calls=%async_computation.9 | async-start | bytes 2359296 | tf_op jit(solution)/shard_map/psum | solution.py:124
  130.8 15.1 %copy-start.3 = (f32[768,768]{1,0:T(8,128)}, f32[768,768]{1,0:T(8,128)S(1)}, u32[]{:S(2)}) copy-start(f32[768,768]{1,0:T(8,128)S(1)} %get-tuple-element.134) | copy-start | bytes 7077892
  130.9 16.4 %copy-start.35 = (bf16[1536,768]{1,0:T(8,128)(2,1)S(1)}, bf16[1536,768]{1,0:T(8,128)(2,1)}, u32[]{:S(2)}) copy-start(bf16[1536,768]{1,0:T(8,128)(2,1)} %param.14) | copy-start | bytes 7077892
  147.3 24.2 %copy-start.31 = (f32[768]{0:T(1024)S(1)}, f32[768]{0:T(1024)}, u32[]{:S(2)}) copy-start(f32[768]{0:T(1024)} %get-tuple-element.119) | copy-start | bytes 9220
  150.3 61.0 %all-reduce.12.cloned.1.call-start = ((), (), s32[]{:S(2)}) async-start(), calls=%async_computation.10 | async-start | bytes 2359296 | tf_op jit(solution)/shard_map/psum | solution.py:139
  179.2 6.6 copy-start.9
  179.2 32.1 %copy-start.26 = (f32[768]{0:T(1024)}, f32[768]{0:T(1024)S(1)}, u32[]{:S(2)}) copy-start(f32[768]{0:T(1024)S(1)} %negate_multiply_fusion.2) | copy-start | bytes 9220
  190.2 25.3 %copy-start.4 = (f32[768,768]{1,0:T(8,128)S(1)}, f32[768,768]{1,0:T(8,128)}, u32[]{:S(2)}) copy-start(f32[768,768]{1,0:T(8,128)} %copy-done.3) | copy-start | bytes 7077892
  190.2 138.3 %reduce-scatter.14.cloned.1.call-start = ((), (), s32[]{:S(2)}) async-start(), calls=%async_computation.11 | async-start | bytes 5898240 | tf_op jit(solution)/shard_map/reduce_scatter | solution.py:177
  219.3 4.5 copy-start.25
  219.3 17.0 %slice-start = ((s8[4718592]{0:T(1024)(128)(4,1)}), s8[524288]{0:T(1024)(128)(4,1)S(1)}, s32[]{:S(2)}) async-start(s8[4718592]{0:T(1024)(128)(4,1)} %bitcast.157), calls=%async_computation.20 | async-start | bytes 1048576
  223.7 12.2 %copy-start.19 = (f32[3,6,64,256]{3,2,1,0:T(8,128)S(1)}, f32[3,6,64,256]{3,2,1,0:T(8,128)}, u32[]{:S(2)}) copy-start(f32[3,6,64,256]{3,2,1,0:T(8,128)} %get-tuple-element.142) | copy-start | bytes 3538948
  223.7 12.5 %slice-start.1 = ((s8[4718592]{0:T(1024)(128)(4,1)}), s8[4194304]{0:T(1024)(128)(4,1)S(1)}, s32[]{:S(2)}) async-start(s8[4718592]{0:T(1024)(128)(4,1)} %bitcast.157), calls=%async_computation.21 | async-start | bytes 8388608
  270.1 103.9 %reduce-scatter.22.cloned.1.call-start = ((), (), s32[]{:S(2)}) async-start(), calls=%async_computation.16 | async-start | bytes 2211840
  341.3 61.4 %reduce-scatter.16.cloned.1.call-start = ((), (), s32[]{:S(2)}) async-start(), calls=%async_computation.13 | async-start | bytes 737280 | tf_op jit(solution)/shard_map/reduce_scatter | solution.py:203
  344.7 98.4 %reduce-scatter.20.cloned.1.call-start = ((), (), s32[]{:S(2)}) async-start(), calls=%async_computation.15 | async-start | bytes 2949120 | tf_op jit(solution)/shard_map/reduce_scatter | solution.py:209
  350.7 132.9 %reduce-scatter.18.cloned.1.call-start = ((), (), s32[]{:S(2)}) async-start(), calls=%async_computation.14 | async-start | bytes 2949120 | tf_op jit(solution)/shard_map/reduce_scatter | solution.py:206
  356.7 154.2 %reduce-scatter.24.cloned.1.call-start = ((), (), s32[]{:S(2)}) async-start(), calls=%async_computation.17 | async-start | bytes 245760
  359.1 178.5 %reduce-scatter.26.cloned.1.call-start = ((), (), s32[]{:S(2)}) async-start(), calls=%async_computation.18 | async-start | bytes 245760
  360.1 200.2 %all-reduce.14.cloned.1.call-start = ((), (), s32[]{:S(2)}) async-start(), calls=%async_computation.12 | async-start | bytes 2359296 | tf_op jit(solution)/shard_map/psum | solution.py:196
  367.5 192.8 %copy-start.6 = (f32[768,768]{1,0:T(8,128)S(1)}, f32[768,768]{1,0:T(8,128)}, u32[]{:S(2)}) copy-start(f32[768,768]{1,0:T(8,128)} %copy-done.5) | copy-start | bytes 7077892
  367.5 279.1 %all-reduce.16.cloned.1.call-start = ((), (), s32[]{:S(2)}) async-start(), calls=%async_computation.19 | async-start | bytes 3833856 | tf_op jit(solution)/shard_map/psum | solution.py:226
  646.6 4.6 copy-start.22
  646.6 6.5 copy-start.1
  646.6 5.7 copy-start.23
  (22 other events, 42.5 us)
Sparse Core Ops, SparseCore 0:
  16.3 59.7 all-gather.1
  108.6 19.7 all-reduce.7
  150.5 20.9 all-reduce.9
  190.3 20.9 all-reduce.11
  270.2 58.2 reduce-scatter.13
  341.4 32.4 reduce-scatter.21
  377.6 25.0 reduce-scatter.15
  405.8 37.3 reduce-scatter.19
  446.2 37.3 reduce-scatter.17
  486.8 23.9 reduce-scatter.23
  513.6 23.9 reduce-scatter.25
  540.4 19.7 all-reduce.13
  563.6 82.8 all-reduce.15
where the time goes:
time: 669 us; the launch traced here: 660 us
  waiting for transfers between devices  416 us (62%)
  matrix products  114 us (17%)
  local copies, waits for them, and re-layouts  49.5 us (7%)
  other arithmetic  41.9 us (6%)
  blocking collectives  21.3 us (3%)
  between operations  14.9 us (2%)
    psum x1, waiting for transfers between devices, on_device(): lax.psum(shares[0].astype(jnp.bfloat16), 'dp').astype(jnp.float32)  83.4 us
    unnamed x16, waiting for transfers between devices  59.7 us
    all_gather x1, waiting for transfers between devices, on_device(): lax.all_gather(packed, 'ctx', axis=1, tiled=True)  48.7 us
    reduce_scatter x1, waiting for transfers between devices, on_device(): lax.psum_scatter(key_term.astype(jnp.bfloat16), 'ctx', scatter_dimension=...  48.6 us
    reduce_scatter x1, waiting for transfers between devices, on_device(): lax.psum_scatter(grad_up.astype(jnp.bfloat16), 'ctx', scatter_dimension=1...  40.5 us
    reduce_scatter x1, waiting for transfers between devices, on_device(): lax.psum_scatter(grad_down.astype(jnp.bfloat16), 'ctx', scatter_dimension...  40.4 us
    reduce_scatter x1, waiting for transfers between devices, on_device(): lax.psum_scatter(grad_proj_out.astype(jnp.bfloat16), 'ctx', scatter_dimen...  26.1 us
    unnamed x93, local copies, waits for them, and re-layouts  24.6 us
  transfers between devices with their start and end apart: 13, of which 13 were waited for; matrix products, arithmetic and copies ran while one was open for 7% of the time, Pallas kernels for 0%

commit v1 on v0

--- a/solution.py
+++ b/solution.py
@@ -7,6 +7,19 @@
 neg_big = -1e30
 dims_rows = (((0,), (0,)), ((), ()))
 dims_cols = (((1,), (1,)), ((), ()))
+
+
+def ring_gather(x, axis, dim):
+    ways = lax.axis_size(axis)
+    up = [(d, (d + 1) % ways) for d in range(ways)]
+    down = [(d, (d - 1) % ways) for d in range(ways)]
+    earlier, later = ([x], [x])
+    for _ in range(ways // 2):
+        earlier.append(lax.ppermute(earlier[-1], axis, up))
+    for _ in range((ways - 1) // 2):
+        later.append(lax.ppermute(later[-1], axis, down))
+    line = jnp.concatenate([*earlier[::-1], *later[1:]], axis=dim)
+    return jnp.roll(line, (lax.axis_index(axis) - ways // 2) * x.shape[dim], axis=dim)
 
 
 def layer_norm(residual, norm_gain, norm_shift):
@@ -62,7 +75,7 @@
     values_own = projected[2].reshape(seq_count, span_rows, local_width)
     packed = jnp.concatenate([keys_own, values_own], axis=-1)
     full_kv, full_seg = (
-        lax.all_gather(packed, "ctx", axis=1, tiled=True),
+        ring_gather(packed, "ctx", 1),
         lax.all_gather(segment_ids, "ctx", axis=1, tiled=True),
     )
     length = full_seg.shape[1]

time: 669 us -> 701 us (1.048)
  blocking collectives: 21.3 us -> 61.9 us
  waiting for transfers between devices: 416 us -> 395 us
  local copies, waits for them, and re-layouts: 49.5 us -> 61.8 us
    all_gather x1 -> x0, waiting for transfers between devices: 48.7 us -> none  [on_device(): lax.all_gather(packed, 'ctx', axis=1, tiled=True)]
    all_gather x1, blocking collectives: 9.6 us -> 50.2 us  [on_device(): lax.all_gather(segment_ids, 'ctx', axis=1, tiled=True)]
    ppermute x0 -> x3, waiting for transfers between devices: none -> 27.2 us  [the longest x2 27.2 us: ring_gather(): earlier.append(lax.ppermute(earlier[-1], axis, up))]
    dynamic_slice x0 -> x2, local copies, waits for them, and re-layouts: none -> 9.16 us  [ring_gather(): jnp.roll(line, (lax.axis_index(axis) - ways // 2) * x.shape[dim], axis=dim)]
    unnamed x93 -> x100, local copies, waits for them, and re-layouts: 24.6 us -> 31.7 us
    unnamed x16 -> x15, waiting for transfers between devices: 59.7 us -> 60.2 us
  transfers between devices with their start and end apart: 13 -> 15, of which waited for: 13 -> 13; matrix products, arithmetic and copies ran while one was open for 7% -> 7% of each run, Pallas kernels for 0% -> 0%
where the time goes in v1:
time: 701 us; the launch traced here: 697 us
  waiting for transfers between devices  395 us (56%)
  matrix products  113 us (16%)
  blocking collectives  61.9 us (9%)
  local copies, waits for them, and re-layouts  61.8 us (9%)
  other arithmetic  42.8 us (6%)
  between operations  15 us (2%)
  starting transfers between devices  7.33 us (1%)
    psum x1, waiting for transfers between devices, on_device(): lax.psum(shares[0].astype(jnp.bfloat16), 'dp').astype(jnp.float32)  82.6 us
    unnamed x15, waiting for transfers between devices  60.2 us
    all_gather x1, blocking collectives, on_device(): lax.all_gather(segment_ids, 'ctx', axis=1, tiled=True)  50.2 us
    reduce_scatter x1, waiting for transfers between devices, on_device(): lax.psum_scatter(key_term.astype(jnp.bfloat16), 'ctx', scatter_dimension=...  47.6 us
    reduce_scatter x1, waiting for transfers between devices, on_device(): lax.psum_scatter(grad_up.astype(jnp.bfloat16), 'ctx', scatter_dimension=1...  40.5 us
    reduce_scatter x1, waiting for transfers between devices, on_device(): lax.psum_scatter(grad_down.astype(jnp.bfloat16), 'ctx', scatter_dimension...  40.5 us
    unnamed x100, local copies, waits for them, and re-layouts  31.7 us
    ppermute x2, waiting for transfers between devices, ring_gather(): earlier.append(lax.ppermute(earlier[-1], axis, up))  27.2 us
  transfers between devices with their start and end apart: 15, of which 13 were waited for; matrix products, arithmetic and copies ran while one was open for 7% of the time, Pallas kernels for 0%

profile of v1, /device:TPU:0, one launch (start us, length us, event | category | flops | bytes accessed | tf_op | source)
XLA Modules:
  0.0 697.2 jit_solution(17883349498684183213)
XLA Ops:
  17.6 27.2 %collective-permute-done = bf16[3,256,768]{2,1,0:T(8,128)(2,1)} collective-permute-done((bf16[3,256,768]{2,1,0:T(8,128)(2,1)}, bf16[3,256,768]{2,1,0:T(8,128)(2,1)}, u32[]{:S(2)}, u32[]{:S(2)}) %collective-permute-start) | collective-permute-done | bytes 1179680 | tf_op jit(solution)/shard_map/ppermute | solution.py:18
  49.8 50.2 %all_gather.3 = s32[3,1024]{1,0:T(4,128)S(1)} all-gather(s32[3,256]{1,0:T(4,128)S(1)} %copy-done.29), channel_id=1, replica_groups=mesh['dp'=4,'ctx'=4,'tensor'=2] {'ctx'}, dimensions={1}, use_global_device_ids=true | all-gather | bytes 15360 | tf_op jit(solution)/shard_map/all_gather | solution.py:79
  112.1 6.7 copy.50
  118.9 5.8 select_reduce_fusion.1
  124.7 6.4 select_reduce_fusion
  131.2 10.0 %bitcast_convert_fusion = (bf16[3,256,6,64]{1,3,2,0:T(8,128)(2,1)S(1)}, f32[3,6,64,256]{3,2,1,0:T(8,128)}) fusion(f32[3,6,256,1024]{3,2,1,0:T(8,128)} %copy-done.1, f32[3,6,256]{2,1,0:T(8,128)S(1)} %log_add_fusion, pred[3,256,1024]{2,1,0:T(8,128)(4,1)S(1)} %copy-done.8, bf16[3,1024,2,6,64]{1,4,3,2,0:T(8,128)(2,1)} %bitcast.155), kind=kOutput, calls=%fused_computation.80 | convolution fusion | flops 623149056 | bytes 23808000 | tf_op jit(solution)/shard_map/while/body/eval_jaxpr/shqk,skhd->sqhd/dot_general | solution.py:118
  146.1 19.4 %all-reduce.8.cloned.1.call-done = bf16[768,768]{1,0:T(8,128)(2,1)} async-done(((bf16[768,768]{1,0:T(8,128)(2,1)}), bf16[768,768]{1,0:T(8,128)(2,1)}) %all-reduce.8.cloned.1.call-update) | async-done | bytes 1179664 | tf_op jit(solution)/shard_map/psum | solution.py:128
  168.0 15.1 %multiply_convert_fusion.2 = (bf16[768,1536]{1,0:T(8,128)(2,1)S(1)}, f32[768,1536]{1,0:T(8,128)}, f32[768,1536]{1,0:T(8,128)}) fusion(bf16[1536,768]{1,0:T(8,128)(2,1)S(1)} %copy-done, f32[768,768]{1,0:T(8,128)S(1)} %get-tuple-element.134, f32[768]{0:T(1024)S(1)} %copy-done.31, f32[768]{0:T(1024)S(1)} %get-tuple-element.144, f32[768]{0:T(1024)S(1)} %fusion.46), kind=kOutput, calls=%fused_computation.10 | convolution fusion | flops 1890975744 | bytes 16524288 | tf_op jit(solution)/shard_map/dot_general | solution.py:135
  187.6 21.1 %all-reduce.10.cloned.1.call-done = bf16[768,768]{1,0:T(8,128)(2,1)} async-done(((bf16[768,768]{1,0:T(8,128)(2,1)}), bf16[768,768]{1,0:T(8,128)(2,1)}) %all-reduce.10.cloned.1.call-update) | async-done | bytes 1179664 | tf_op jit(solution)/shard_map/psum | solution.py:137
  216.4 6.5 add_convert_fusion
  227.7 20.9 %all-reduce.12.cloned.1.call-done = bf16[768,768]{1,0:T(8,128)(2,1)} async-done(((bf16[768,768]{1,0:T(8,128)(2,1)}), bf16[768,768]{1,0:T(8,128)(2,1)}) %all-reduce.12.cloned.1.call-update) | async-done | bytes 1179664 | tf_op jit(solution)/shard_map/psum | solution.py:152
  248.6 4.2 fusion.55
  260.8 12.2 %convolution_convert_fusion.2 = bf16[3,6,64,1024]{3,2,1,0:T(8,128)(2,1)} fusion(bf16[3,256,6,64]{1,0,3,2:T(4,128)(2,1)} %reshape.160, f32[3,6,256,1024]{3,2,1,0:T(8,128)} %copy-done.1, f32[3,6,256]{2,1,0:T(8,128)S(1)} %copy-done.26, pred[3,256,1024]{2,1,0:T(8,128)(4,1)} %broadcast_compare_fusion), kind=kOutput, calls=%fused_computation.55 | convolution fusion | flops 624033792 | bytes 22628352 | tf_op jit(solution)/shard_map/while/body/eval_jaxpr/shqk,sqhd->kshd/dot_general | solution.py:58
  273.3 13.0 %multiply_convert_fusion = bf16[3,6,256,1024]{3,2,1,0:T(8,128)(2,1)} fusion(f32[3,6,256,1024]{3,2,1,0:T(8,128)} %copy-done.1, f32[3,6,256]{2,1,0:T(8,128)S(1)} %fusion.25, f32[3,6,256]{2,1,0:T(8,128)S(1)} %copy-done.26, pred[3,256,1024]{2,1,0:T(8,128)(4,1)} %broadcast_compare_fusion, bf16[3,1024,2,6,64]{1,4,3,2,0:T(8,128)(2,1)S(1)} %bitcast.159, ...), kind=kOutput, calls=%fused_computation | convolution fusion | flops 632291328 | bytes 32096256 | tf_op jit(solution)/shard_map/while/body/eval_jaxpr/sqhd,skhd->shqk/dot_general | solution.py:47
  286.4 7.2 %multiply_convert_fusion.1 = bf16[3,6,64,1024]{3,2,1,0:T(8,128)(2,1)} fusion(bf16[3,6,256,1024]{3,2,1,0:T(8,128)(2,1)} %multiply_convert_fusion, bf16[3,256,6,64]{1,0,3,2:T(4,128)(2,1)} %reshape_squeeze.11), kind=kOutput, calls=%fused_computation.8 | convolution fusion | flops 606339072 | bytes 12386304 | tf_op jit(solution)/shard_map/while/body/eval_jaxpr/shqk,sqhd->kshd/dot_general | solution.py:56
  293.6 4.3 copy.60
  297.8 4.3 copy.61
  302.2 5.0 pad_maximum_fusion
  307.7 7.4 %fusion.19 = bf16[3,6,64,256]{3,2,1,0:T(8,128)(2,1)S(1)} fusion(bf16[3,6,256,1024]{3,2,1,0:T(8,128)(2,1)} %multiply_convert_fusion, bf16[3,1024,2,6,64]{1,4,3,2,0:T(8,128)(2,1)} %bitcast.156), kind=kOutput, calls=%fused_computation.66 | convolution fusion | flops 604569600 | bytes 12386304 | tf_op jit(solution)/shard_map/while/body/eval_jaxpr/shqk,skhd->sqhd/dot_general | solution.py:173
  318.1 47.6 %reduce-scatter.14.cloned.1.call-done = bf16[256,3,2,384]{3,0,1,2:T(8,128)(2,1)} async-done(((bf16[1024,3,2,384]{3,0,1,2:T(8,128)(2,1)}), bf16[256,3,2,384]{3,0,1,2:T(8,128)(2,1)}) %reduce-scatter.14.cloned.1.call-update) | async-done | bytes 1179664 | tf_op jit(solution)/shard_map/reduce_scatter | solution.py:190
  369.6 5.2 copy.76
  381.5 5.9 convolution_convert_fusion
  388.1 6.1 convolution_convert_fusion.1
  404.3 6.3 reduce-scatter.22.cloned.1.call-done
  413.4 25.9 %reduce-scatter.16.cloned.1.call-done = bf16[384,192]{0,1:T(8,128)(2,1)} async-done(((bf16[384,768]{0,1:T(8,128)(2,1)}), bf16[384,192]{0,1:T(8,128)(2,1)}) %reduce-scatter.16.cloned.1.call-update) | async-done | bytes 147472 | tf_op jit(solution)/shard_map/reduce_scatter | solution.py:216
  439.3 40.5 %reduce-scatter.20.cloned.1.call-done = bf16[1536,192]{0,1:T(8,128)(2,1)} async-done(((bf16[1536,768]{0,1:T(8,128)(2,1)}), bf16[1536,192]{0,1:T(8,128)(2,1)}) %reduce-scatter.20.cloned.1.call-update) | async-done | bytes 589840 | tf_op jit(solution)/shard_map/reduce_scatter | solution.py:222
  479.8 40.5 %reduce-scatter.18.cloned.1.call-done = bf16[1536,192]{0,1:T(8,128)(2,1)} async-done(((bf16[1536,768]{0,1:T(8,128)(2,1)}), bf16[1536,192]{0,1:T(8,128)(2,1)}) %reduce-scatter.18.cloned.1.call-update) | async-done | bytes 589840 | tf_op jit(solution)/shard_map/reduce_scatter | solution.py:219
  520.3 27.3 %reduce-scatter.24.cloned.1.call-done = bf16[192,2]{1,0:T(8,128)(2,1)} async-done(((bf16[768,2]{1,0:T(8,128)(2,1)}), bf16[192,2]{1,0:T(8,128)(2,1)}) %reduce-scatter.24.cloned.1.call-update) | async-done | bytes 784
  548.5 26.3 %reduce-scatter.26.cloned.1.call-done = bf16[192,2]{1,0:T(8,128)(2,1)} async-done(((bf16[768,2]{1,0:T(8,128)(2,1)}), bf16[192,2]{1,0:T(8,128)(2,1)}) %reduce-scatter.26.cloned.1.call-update) | async-done | bytes 784
  575.7 11.7 %all-reduce = (bf16[2,192]{1,0:T(2,128)(2,1)S(1)}, bf16[2,192]{1,0:T(2,128)(2,1)S(1)}) all-reduce(bf16[2,192]{1,0:T(2,128)(2,1)S(1)} %copy.79, bf16[2,192]{1,0:T(2,128)(2,1)S(1)} %copy.81), channel_id=1, replica_groups=mesh['dp'=4,'ctx'=4,'tensor'=2] {'dp'}, use_global_device_ids=true, to_apply=%region_26.27 | all-reduce | flops 768 | bytes 3072 | tf_op jit(solution)/shard_map/psum | solution.py:243
  588.5 9.0 %all-reduce.14.cloned.1.call-done = bf16[3,256,768]{2,1,0:T(8,128)(2,1)} async-done(((bf16[3,256,768]{2,1,0:T(8,128)(2,1)}), bf16[3,256,768]{2,1,0:T(8,128)(2,1)}) %all-reduce.14.cloned.1.call-update) | async-done | bytes 1179664 | tf_op jit(solution)/shard_map/psum | solution.py:209
  601.2 82.6 %all-reduce.16.cloned.1.call-done = (bf16[3,192,384]{1,2,0:T(8,128)(2,1)}, bf16[384,192]{0,1:T(8,128)(2,1)}, bf16[1536,192]{0,1:T(8,128)(2,1)}, bf16[1536,192]{0,1:T(8,128)(2,1)}) async-done(((bf16[3,192,384]{1,2,0:T(8,128)(2,1)}, bf16[384,192]{0,1:T(8,128)(2,1)}, bf16[1536,192]{0,1:T(8,128)(2,1)}, bf16[1536,192]{0,1:T(8,128)(2,1)}), (bf16[3,192,384]{1,2,0:T(8,128)(2,1)}, bf16[384,192]{0,1:T(8,128)(2,1)}, ...) | async-done | bytes 1769488 | tf_op jit(solution)/shard_map/psum | solution.py:239
  (190 shorter events, 100.2 us)
Async XLA Ops:
  7.2 160.8 %copy-start = (bf16[1536,768]{1,0:T(8,128)(2,1)S(1)}, bf16[1536,768]{1,0:T(8,128)(2,1)}, u32[]{:S(2)}) copy-start(bf16[1536,768]{1,0:T(8,128)(2,1)} %param.13) | copy-start | bytes 7077892
  7.2 158.4 %all-reduce.8.cloned.1.call-start = ((), (), s32[]{:S(2)}) async-start(), calls=%async_computation.7 | async-start | bytes 2359296 | tf_op jit(solution)/shard_map/psum | solution.py:128
  12.2 37.6 %copy-start.29 = (s32[3,256]{1,0:T(4,128)S(1)}, s32[3,256]{1,0:T(4,128)}, u32[]{:S(2)}) copy-start(s32[3,256]{1,0:T(4,128)} %param.10) | copy-start | bytes 9220
  14.7 30.2 %collective-permute-start = (bf16[3,256,768]{2,1,0:T(8,128)(2,1)}, bf16[3,256,768]{2,1,0:T(8,128)(2,1)}, u32[]{:S(2)}, u32[]{:S(2)}) collective-permute-start(bf16[3,256,768]{2,1,0:T(8,128)(2,1)} %pad_maximum_fusion.2), channel_id=1, source_target_pairs={{0,2},{2,4},{4,6},{6,0},{1,3},{3,5},{5,7},{7,1},{8,10},{10,12},{12... | collective-permute-start | bytes 3538952 | tf_op jit(solution)/shard_map/ppermute | solution.py:18
  44.9 56.5 %collective-permute-start.1 = (bf16[3,256,768]{2,1,0:T(8,128)(2,1)}, bf16[3,256,768]{2,1,0:T(8,128)(2,1)}, u32[]{:S(2)}, u32[]{:S(2)}) collective-permute-start(bf16[3,256,768]{2,1,0:T(8,128)(2,1)} %collective-permute-done), channel_id=1, source_target_pairs={{0,2},{2,4},{4,6},{6,0},{1,3},{3,5},{5,7},{7,1},{8,10},{10,12},{12... | collective-permute-start | bytes 3538952 | tf_op jit(solution)/shard_map/ppermute | solution.py:18
  45.7 58.5 %collective-permute-start.2 = (bf16[3,256,768]{2,1,0:T(8,128)(2,1)}, bf16[3,256,768]{2,1,0:T(8,128)(2,1)}, u32[]{:S(2)}, u32[]{:S(2)}) collective-permute-start(bf16[3,256,768]{2,1,0:T(8,128)(2,1)} %pad_maximum_fusion.2), channel_id=1, source_target_pairs={{0,6},{2,0},{4,2},{6,4},{1,7},{3,1},{5,3},{7,5},{8,14},{10,8},{12,... | collective-permute-start | bytes 3538952 | tf_op jit(solution)/shard_map/ppermute | solution.py:20
  112.1 6.7 copy-start.8
  124.7 6.5 copy-start.1
  131.1 10.1 %copy-start.25 = (f32[3,6,256]{2,1,0:T(8,128)}, f32[3,6,256]{2,1,0:T(8,128)S(1)}, u32[]{:S(2)}) copy-start(f32[3,6,256]{2,1,0:T(8,128)S(1)} %log_add_fusion) | copy-start | bytes 55300
  141.7 23.8 %copy-start.11 = (bf16[3,256,768]{2,1,0:T(8,128)(2,1)S(1)}, bf16[3,256,768]{2,1,0:T(8,128)(2,1)}, u32[]{:S(2)}) copy-start(bf16[3,256,768]{2,1,0:T(8,128)(2,1)} %param.9) | copy-start | bytes 3538948
  144.5 64.2 %all-reduce.10.cloned.1.call-start = ((), (), s32[]{:S(2)}) async-start(), calls=%async_computation.8 | async-start | bytes 2359296 | tf_op jit(solution)/shard_map/psum | solution.py:137
  168.0 15.1 %copy-start.2 = (f32[768,768]{1,0:T(8,128)}, f32[768,768]{1,0:T(8,128)S(1)}, u32[]{:S(2)}) copy-start(f32[768,768]{1,0:T(8,128)S(1)} %get-tuple-element.134) | copy-start | bytes 7077892
  168.0 16.5 %copy-start.36 = (bf16[1536,768]{1,0:T(8,128)(2,1)S(1)}, bf16[1536,768]{1,0:T(8,128)(2,1)}, u32[]{:S(2)}) copy-start(bf16[1536,768]{1,0:T(8,128)(2,1)} %param.14) | copy-start | bytes 7077892
  184.5 24.2 %copy-start.32 = (f32[768]{0:T(1024)S(1)}, f32[768]{0:T(1024)}, u32[]{:S(2)}) copy-start(f32[768]{0:T(1024)} %get-tuple-element.119) | copy-start | bytes 9220
  187.5 61.0 %all-reduce.12.cloned.1.call-start = ((), (), s32[]{:S(2)}) async-start(), calls=%async_computation.9 | async-start | bytes 2359296 | tf_op jit(solution)/shard_map/psum | solution.py:152
  216.4 6.6 copy-start.7
  216.4 32.2 %copy-start.27 = (f32[768]{0:T(1024)}, f32[768]{0:T(1024)S(1)}, u32[]{:S(2)}) copy-start(f32[768]{0:T(1024)S(1)} %negate_multiply_fusion.2) | copy-start | bytes 9220
  227.4 138.2 %reduce-scatter.14.cloned.1.call-start = ((), (), s32[]{:S(2)}) async-start(), calls=%async_computation.10 | async-start | bytes 5898240 | tf_op jit(solution)/shard_map/reduce_scatter | solution.py:190
  256.4 16.9 %slice-start = ((s8[4718592]{0:T(1024)(128)(4,1)}), s8[524288]{0:T(1024)(128)(4,1)S(1)}, s32[]{:S(2)}) async-start(s8[4718592]{0:T(1024)(128)(4,1)} %bitcast.157), calls=%async_computation.19 | async-start | bytes 1048576
  260.8 12.2 %copy-start.19 = (f32[3,6,64,256]{3,2,1,0:T(8,128)S(1)}, f32[3,6,64,256]{3,2,1,0:T(8,128)}, u32[]{:S(2)}) copy-start(f32[3,6,64,256]{3,2,1,0:T(8,128)} %get-tuple-element.142) | copy-start | bytes 3538948
  260.8 12.5 %slice-start.1 = ((s8[4718592]{0:T(1024)(128)(4,1)}), s8[4194304]{0:T(1024)(128)(4,1)S(1)}, s32[]{:S(2)}) async-start(s8[4718592]{0:T(1024)(128)(4,1)} %bitcast.157), calls=%async_computation.20 | async-start | bytes 8388608
  307.2 103.4 %reduce-scatter.22.cloned.1.call-start = ((), (), s32[]{:S(2)}) async-start(), calls=%async_computation.15 | async-start | bytes 2211840
  378.0 61.2 %reduce-scatter.16.cloned.1.call-start = ((), (), s32[]{:S(2)}) async-start(), calls=%async_computation.12 | async-start | bytes 737280 | tf_op jit(solution)/shard_map/reduce_scatter | solution.py:216
  381.4 98.3 %reduce-scatter.20.cloned.1.call-start = ((), (), s32[]{:S(2)}) async-start(), calls=%async_computation.14 | async-start | bytes 2949120 | tf_op jit(solution)/shard_map/reduce_scatter | solution.py:222
  387.4 132.8 %reduce-scatter.18.cloned.1.call-start = ((), (), s32[]{:S(2)}) async-start(), calls=%async_computation.13 | async-start | bytes 2949120 | tf_op jit(solution)/shard_map/reduce_scatter | solution.py:219
  394.2 153.4 %reduce-scatter.24.cloned.1.call-start = ((), (), s32[]{:S(2)}) async-start(), calls=%async_computation.16 | async-start | bytes 245760
  396.3 5.1 copy-start.18
  398.0 176.8 %reduce-scatter.26.cloned.1.call-start = ((), (), s32[]{:S(2)}) async-start(), calls=%async_computation.17 | async-start | bytes 245760
  398.9 198.6 %all-reduce.14.cloned.1.call-start = ((), (), s32[]{:S(2)}) async-start(), calls=%async_computation.11 | async-start | bytes 2359296 | tf_op jit(solution)/shard_map/psum | solution.py:209
  404.3 279.5 %all-reduce.16.cloned.1.call-start = ((), (), s32[]{:S(2)}) async-start(), calls=%async_computation.18 | async-start | bytes 3833856 | tf_op jit(solution)/shard_map/psum | solution.py:239
  683.8 4.5 copy-start.23
  683.8 5.6 copy-start.24
  (25 other events, 50.7 us)
Sparse Core Ops, SparseCore 0:
  144.6 20.8 all-reduce.7
  187.7 20.9 all-reduce.9
  227.6 20.9 all-reduce.11
  307.3 58.2 reduce-scatter.13
  378.2 32.4 reduce-scatter.21
  414.2 25.0 reduce-scatter.15
  442.3 37.3 reduce-scatter.19
  482.8 37.3 reduce-scatter.17
  523.6 23.9 reduce-scatter.23
  550.8 23.9 reduce-scatter.25
  577.7 19.7 all-reduce.13
  600.8 82.8 all-reduce.15
